TPU v7x, 32 devices: a whole 2x2x4 slice. The times are simulated.
32 devices in a mesh: lon: 8 (over y, x, core), depth: 4 (over z).
Axes of the slice: x: 2, y: 2, z: 4, core: 2. Of those that a mesh axis runs over, the one named last changes fastest.
Arguments:
- innovations: float32 [5, 256, 128, 256], P(None, 'depth', 'lon'), may hold values from -6 to 6
- courant: float32 [3, 256, 128, 256], P(None, 'depth', 'lon'), may hold values from -0.3 to 0.3
- diffusivity: float32 [256, 128, 256], P('depth', 'lon'), may hold values from 0.05 to 0.12
- sea_bricks: int32 [256, 8, 128], P('depth', 'lon'), may hold values 0 or 1
- tile_ranks: int32 [8, 8], P('lon'), may hold values from 16 to 128
- row_factors: bfloat16 [8, 8, 4096, 128], P('lon', None, None, 'depth'), may hold values from -0.09375 to 0.09375
- column_factors: bfloat16 [8, 8, 4096, 128], P('lon', None, None, 'depth'), may hold values from -0.25 to 0.25
Outputs:
- initial_adjoint: float32 [256, 128, 256], P('depth', 'lon')
- gradient: float32 [256, 128, 256], P('depth', 'lon')
All inputs are finite; a program needn't handle non-finite values. No bound on the sum of `sea_bricks` on one device may be relied on, other than what follows from the above.
Results may differ from a plain program's by a relative error of at most 0.0041.
Values may be sent and summed in bfloat16 or wider, within the bound.
No kernel may reach another device: no remote copies, remote signals or barrier semaphores. Data moves between devices by JAX's collectives and lax.ppermute only.
A program may use at most 64 MiB of HBM per device.

v0:
```python
import jax
import jax.numpy as jnp
from jax import lax
from jax.sharding import PartitionSpec as P


def from_behind(value, axis, steps):
    count = lax.axis_size(axis)
    initial, last = (max(0, -steps), min(count, count - steps))
    return lax.ppermute(value, axis, [(source, source + steps) for source in range(initial, last)])


def shifted(block, axis, distance):
    devices = range(lax.axis_size(axis))
    route = [((i - distance) % len(devices), i) for i in devices]
    return lax.ppermute(block, axis, route)


def lat_terms(plus_term, minus_term):
    lower = jnp.pad(plus_term[:, :, :-1], ((0, 0), (0, 0), (1, 0)))
    upper = jnp.pad(minus_term[:, :, 1:], ((0, 0), (0, 0), (0, 1)))
    return lower + upper


def per_device(
    innovations, courant, diffusivity, sea_bricks, tile_ranks, row_factors, column_factors
):
    levels_here, lon_cells, lat_cells = diffusivity.shape
    tile_cols = lon_cells * lat_cells
    blocks_row = tile_ranks.shape[1]
    sea = sea_bricks.astype(jnp.float32)
    sea = jnp.broadcast_to(sea[:, :, :, None], (levels_here, 1, lat_cells // 2, 2)).reshape(
        levels_here, 1, lat_cells
    )
    plus = diffusivity[None] - 0.5 * courant
    minus = diffusivity[None] + 0.5 * courant
    center = 1.0 - 6.0 * diffusivity
    steps_total = innovations.shape[0] - 1
    lam = sea * innovations[steps_total]
    for step in reversed(range(steps_total)):
        plus_term = plus * lam
        minus_term = minus * lam
        below = from_behind(plus_term[0, -1:], "depth", 1)
        above = from_behind(minus_term[0, :1], "depth", -1)
        west = shifted(plus_term[1][:, -1:], "lon", 1)
        east = shifted(minus_term[1][:, :1], "lon", -1)
        out = center * lam
        out = out + jnp.concatenate([below, plus_term[0, :-1]], 0)
        out = out + jnp.concatenate([minus_term[0, 1:], above], 0)
        out = out + jnp.concatenate([west, plus_term[1][:, :-1]], 1)
        out = out + jnp.concatenate([minus_term[1][:, 1:], east], 1)
        lam = sea * (out + lat_terms(plus_term[2], minus_term[2]) + innovations[step])
    lam_half = lam.astype(jnp.bfloat16).reshape(levels_here, tile_cols)
    ranks = tile_ranks[0]
    all_levels = lax.all_gather(lam_half, "depth", axis=0, tiled=True)
    left = row_factors[0]
    width = left.shape[2]
    columns = lax.axis_index("depth") * width + jnp.arange(width, dtype=jnp.int32)
    coeff = jnp.einsum("zt,ktr->kzr", all_levels, left, preferred_element_type=jnp.float32)
    keep = (columns[None, :] < ranks[:, None]).astype(jnp.float32)
    coeff = (coeff * keep[:, None, :]).astype(jnp.bfloat16)
    pieces = []
    for slot in range(blocks_row):
        pieces.append(shifted(coeff[slot], "lon", slot - blocks_row // 2))
    received = jnp.stack(pieces, 0)
    right = column_factors[0]
    gradient = lax.psum_scatter(
        jnp.einsum("kzr,ktr->zt", received, right, preferred_element_type=jnp.float32),
        "depth",
        scatter_dimension=0,
        tiled=True,
    )
    return (lam, gradient.reshape(levels_here, lon_cells, lat_cells))


def solution(mesh):
    placed = (
        P(None, "depth", "lon", None),
        P(None, "depth", "lon", None),
        P("depth", "lon", None),
        P("depth", "lon", None),
        P("lon", None),
        P("lon", None, None, "depth"),
        P("lon", None, None, "depth"),
    )
    return jax.shard_map(
        per_device,
        mesh=mesh,
        in_specs=placed,
        out_specs=(P("depth", "lon", None), P("depth", "lon", None)),
        check_vma=False,
    )
```

profile of v0, /device:TPU:0, one launch (start us, length us, event | category | flops | bytes accessed | tf_op | source)
XLA Modules:
  0.0 223.0 jit_solution(1263880004125982278)
XLA Ops:
  7.2 1.0 convert_element_type.29
  8.4 1.4 multiply_bitcast_fusion
  9.8 2.8 %fusion.8 = (f32[3,64,16,256]{3,2,1,0:T(8,128)S(1)}, f32[3,64,16,256]{3,2,1,0:T(8,128)S(1)}) fusion(f32[3,64,16,256]{3,2,1,0:T(8,128)} %param.8, f32[64,16,256]{2,1,0:T(8,128)S(1)} %multiply_bitcast_fusion, f32[64,16,256]{2,1,0:T(8,128)S(1)} %copy-done.1), kind=kLoop, calls=%fused_computation.11 | loop fusion | flops 3932160 | bytes 11534336 | tf_op jit(solution)/shard_map/mul | solution.py:42
  12.7 5.0 %collective-permute-start = (f32[1,16,256]{2,1,0:T(8,128)S(1)}, f32[1,16,256]{2,1,0:T(8,128)S(1)}, u32[]{:S(2)}, u32[]{:S(2)}) collective-permute-start(f32[1,16,256]{2,1,0:T(8,128)S(1)} %slice_bitcast_fusion.39), channel_id=1, source_target_pairs={{0,1},{1,2},{2,3},{4,5},{5,6},{6,7},{8,9},{9,10},{10,11},{12,13},{... | collective-permute-start | bytes 49160 | tf_op jit(solution)/shard_map/ppermute | solution.py:10
  17.7 1.3 collective-permute-start.1
  19.0 0.5 slice_bitcast_fusion.12
  19.6 2.7 %collective-permute-start.3 = (f32[64,1,256]{2,1,0:T(1,128)S(1)}, f32[64,1,256]{2,1,0:T(1,128)S(1)}, u32[]{:S(2)}, u32[]{:S(2)}) collective-permute-start(f32[64,1,256]{2,1,0:T(1,128)S(1)} %slice.293), channel_id=1, source_target_pairs={{4,0},{8,4},{12,8},{16,12},{20,16},{24,20},{28,24},{0,28},{5,1},{9... | collective-permute-start | bytes 196616 | tf_op jit(solution)/shard_map/ppermute | solution.py:16
  22.6 0.3 slice.297
  23.3 0.9 collective-permute-done.2
  24.2 1.3 fusion.14
  25.5 0.6 copy-done.2
  26.1 1.0 fusion.7
  27.6 4.5 %collective-permute-start.4 = (f32[1,16,256]{2,1,0:T(8,128)S(1)}, f32[1,16,256]{2,1,0:T(8,128)S(1)}, u32[]{:S(2)}, u32[]{:S(2)}) collective-permute-start(f32[1,16,256]{2,1,0:T(8,128)S(1)} %slice_bitcast_fusion.37), channel_id=1, source_target_pairs={{0,1},{1,2},{2,3},{4,5},{5,6},{6,7},{8,9},{9,10},{10,11},{12,13},{... | collective-permute-start | bytes 49160 | tf_op jit(solution)/shard_map/ppermute | solution.py:10
  32.1 1.3 collective-permute-start.5
  33.5 2.5 %collective-permute-start.7 = (f32[64,1,256]{2,1,0:T(1,128)S(1)}, f32[64,1,256]{2,1,0:T(1,128)S(1)}, u32[]{:S(2)}, u32[]{:S(2)}) collective-permute-start(f32[64,1,256]{2,1,0:T(1,128)S(1)} %slice.307), channel_id=1, source_target_pairs={{4,0},{8,4},{12,8},{16,12},{20,16},{24,20},{28,24},{0,28},{5,1},{9... | collective-permute-start | bytes 196616 | tf_op jit(solution)/shard_map/ppermute | solution.py:16
  36.6 1.2 collective-permute-done.5
  37.8 2.8 %collective-permute-done.6 = f32[64,1,256]{2,1,0:T(1,128)S(1)} collective-permute-done((f32[64,1,256]{2,1,0:T(1,128)S(1)}, f32[64,1,256]{2,1,0:T(1,128)S(1)}, u32[]{:S(2)}, u32[]{:S(2)}) %collective-permute-start.6) | collective-permute-done | bytes 65568 | tf_op jit(solution)/shard_map/ppermute | solution.py:16
  40.6 1.2 fusion.20
  41.9 1.0 fusion.6
  43.3 4.3 %collective-permute-start.8 = (f32[1,16,256]{2,1,0:T(8,128)S(1)}, f32[1,16,256]{2,1,0:T(8,128)S(1)}, u32[]{:S(2)}, u32[]{:S(2)}) collective-permute-start(f32[1,16,256]{2,1,0:T(8,128)S(1)} %slice_bitcast_fusion.35), channel_id=1, source_target_pairs={{0,1},{1,2},{2,3},{4,5},{5,6},{6,7},{8,9},{9,10},{10,11},{12,13},{... | collective-permute-start | bytes 49160 | tf_op jit(solution)/shard_map/ppermute | solution.py:10
  47.6 1.3 collective-permute-start.9
  49.1 0.5 collective-permute-start.10
  50.2 3.1 %collective-permute-done.9 = f32[1,16,256]{2,1,0:T(8,128)S(1)} collective-permute-done((f32[1,16,256]{2,1,0:T(8,128)S(1)}, f32[1,16,256]{2,1,0:T(8,128)S(1)}, u32[]{:S(2)}, u32[]{:S(2)}) %collective-permute-start.9) | collective-permute-done | bytes 16416 | tf_op jit(solution)/shard_map/ppermute | solution.py:10
  53.3 0.5 collective-permute-done.10
  53.7 1.2 fusion.26
  55.0 1.1 fusion.1
  56.6 1.3 collective-permute-start.13
  57.9 5.4 %collective-permute-start.12 = (f32[1,16,256]{2,1,0:T(8,128)S(1)}, f32[1,16,256]{2,1,0:T(8,128)S(1)}, u32[]{:S(2)}, u32[]{:S(2)}) collective-permute-start(f32[1,16,256]{2,1,0:T(8,128)S(1)} %slice_bitcast_fusion.33), channel_id=1, source_target_pairs={{0,1},{1,2},{2,3},{4,5},{5,6},{6,7},{8,9},{9,10},{10,11},{12,13},{... | collective-permute-start | bytes 49160 | tf_op jit(solution)/shard_map/ppermute | solution.py:10
  63.5 2.7 %collective-permute-start.15 = (f32[64,1,256]{2,1,0:T(1,128)S(1)}, f32[64,1,256]{2,1,0:T(1,128)S(1)}, u32[]{:S(2)}, u32[]{:S(2)}) collective-permute-start(f32[64,1,256]{2,1,0:T(1,128)S(1)} %slice.335), channel_id=1, source_target_pairs={{4,0},{8,4},{12,8},{16,12},{20,16},{24,20},{28,24},{0,28},{5,1},{9... | collective-permute-start | bytes 196616 | tf_op jit(solution)/shard_map/ppermute | solution.py:16
  66.7 1.4 collective-permute-done.14
  68.1 2.2 fusion.35
  70.3 1.0 copy.12
  71.5 46.6 %all-gather.2.cloned.1.call-done = bf16[256,4096]{1,0:T(8,128)(2,1)} async-done(((bf16[64,4096]{1,0:T(8,128)(2,1)}), bf16[256,4096]{1,0:T(8,128)(2,1)}) %all-gather.2.cloned.1.call-update) | async-done | bytes 2097168 | tf_op jit(solution)/shard_map/all_gather | solution.py:55
  118.1 2.5 %fusion.37 = f32[256,256]{0,1:S(1)} fusion(bf16[256,4096]{1,0:T(8,128)(2,1)} %all-gather.2.cloned.1.call-done, bf16[4096,256]{0,1:T(8,128)(2,1)S(1)} %bitcast.144), kind=kOutput, calls=%fused_computation.97 | convolution fusion | flops 536870912 | bytes 4456448
  120.7 1.5 collective-permute-start.16
  122.2 0.5 collective-permute-start.23
  122.7 1.0 collective-permute-start.22
  123.7 0.4 collective-permute-start.21
  124.1 0.4 collective-permute-done.16
  124.5 1.4 collective-permute-start.17
  125.9 1.7 collective-permute-done.17
  127.7 3.4 %collective-permute-start.18 = (bf16[256,32]{0,1:T(8,128)(2,1)S(1)}, bf16[256,32]{0,1:T(8,128)(2,1)S(1)}, u32[]{:S(2)}, u32[]{:S(2)}) collective-permute-start(bf16[256,32]{0,1:T(8,128)(2,1)S(1)} %get-tuple-element.33), channel_id=1, source_target_pairs={{8,0},{12,4},{16,8},{20,12},{24,16},{28,20},{0,24},{4,28},{9,1},{1... | collective-permute-start | bytes 49160 | tf_op jit(solution)/shard_map/ppermute | solution.py:16
  131.1 1.4 collective-permute-done.18
  132.5 0.5 collective-permute-start.19
  133.0 1.4 collective-permute-done.19
  134.5 2.7 %convolution_bitcast_fusion = f32[256,4096]{1,0:T(8,128)} fusion(bf16[8,256,32]{1,2,0:T(8,128)(2,1)S(1)} %constant_dynamic-update-slice_fusion, bf16[1,8,4096,32]{2,3,1,0:T(8,128)(2,1)S(1)} %copy-done.3), kind=kOutput, calls=%fused_computation | convolution fusion | flops 536870912 | bytes 6422528 | tf_op jit(solution)/shard_map/kzr,ktr->zt/dot_general | solution.py:68
  137.3 76.4 %reduce-scatter.2.cloned.1.call-done = f32[64,4096]{1,0:T(8,128)} async-done(((f32[256,4096]{1,0:T(8,128)}), f32[64,4096]{1,0:T(8,128)}) %reduce-scatter.2.cloned.1.call-update) | async-done | bytes 1048592 | tf_op jit(solution)/shard_map/reduce_scatter | solution.py:67
  213.7 2.5 %copy.13 = f32[8,8,16,256]{3,2,1,0:T(8,128)} copy(f32[8,8,16,256]{3,1,2,0:T(8,128)} %bitcast.159) | data formatting | bytes 2097152
  (88 shorter events, 4.8 us)
Async XLA Ops:
  7.2 110.9 %copy-start = (bf16[1,8,4096,32]{2,3,1,0:T(8,128)(2,1)S(1)}, bf16[1,8,4096,32]{2,3,1,0:T(8,128)(2,1)}, u32[]{:S(2)}) copy-start(bf16[1,8,4096,32]{2,3,1,0:T(8,128)(2,1)} %param.12) | copy-start | bytes 6291460
  7.2 2.6 %copy-start.1 = (f32[64,16,256]{2,1,0:T(8,128)S(1)}, f32[64,16,256]{2,1,0:T(8,128)}, u32[]{:S(2)}) copy-start(f32[64,16,256]{2,1,0:T(8,128)} %param.9) | copy-start | bytes 3145732
  7.2 110.9 %all-gather.2.cloned.1.call-start = ((), (), s32[]{:S(2)}) async-start(), calls=%async_computation.1 | async-start | bytes 2621440 | tf_op jit(solution)/shard_map/all_gather | solution.py:55
  12.7 10.3 %collective-permute-start = (f32[1,16,256]{2,1,0:T(8,128)S(1)}, f32[1,16,256]{2,1,0:T(8,128)S(1)}, u32[]{:S(2)}, u32[]{:S(2)}) collective-permute-start(f32[1,16,256]{2,1,0:T(8,128)S(1)} %slice_bitcast_fusion.39), channel_id=1, source_target_pairs={{0,1},{1,2},{2,3},{4,5},{5,6},{6,7},{8,9},{9,10},{10,11},{12,13},{... | collective-permute-start | bytes 49160 | tf_op jit(solution)/shard_map/ppermute | solution.py:10
  17.7 5.6 %collective-permute-start.1 = (f32[1,16,256]{2,1,0:T(8,128)S(1)}, f32[1,16,256]{2,1,0:T(8,128)S(1)}, u32[]{:S(2)}, u32[]{:S(2)}) collective-permute-start(f32[1,16,256]{2,1,0:T(8,128)S(1)} %slice_bitcast_fusion.38), channel_id=1, source_target_pairs={{1,0},{2,1},{3,2},{5,4},{6,5},{7,6},{9,8},{10,9},{11,10},{13,12},{... | collective-permute-start | bytes 49160 | tf_op jit(solution)/shard_map/ppermute | solution.py:10
  19.0 5.3 %slice-start = ((s8[5242880]{0:T(1024)(128)(4,1)}), s8[4194304]{0:T(1024)(128)(4,1)S(1)}, s32[]{:S(2)}) async-start(s8[5242880]{0:T(1024)(128)(4,1)} %bitcast.145), calls=%async_computation.3 | async-start | bytes 8388608
  19.4 4.8 %slice-start.1 = ((s8[5242880]{0:T(1024)(128)(4,1)}), s8[1048576]{0:T(1024)(128)(4,1)S(1)}, s32[]{:S(2)}) async-start(s8[5242880]{0:T(1024)(128)(4,1)} %bitcast.145), calls=%async_computation.4 | async-start | bytes 2097152
  19.5 4.6 %collective-permute-start.2 = (f32[64,1,256]{2,1,0:T(1,128)S(1)}, f32[64,1,256]{2,1,0:T(1,128)S(1)}, u32[]{:S(2)}, u32[]{:S(2)}) collective-permute-start(f32[64,1,256]{2,1,0:T(1,128)S(1)} %slice.289), channel_id=1, source_target_pairs={{28,0},{0,4},{4,8},{8,12},{12,16},{16,20},{20,24},{24,28},{29,1},{... | collective-permute-start | bytes 196616 | tf_op jit(solution)/shard_map/ppermute | solution.py:16
  19.6 4.6 %collective-permute-start.3 = (f32[64,1,256]{2,1,0:T(1,128)S(1)}, f32[64,1,256]{2,1,0:T(1,128)S(1)}, u32[]{:S(2)}, u32[]{:S(2)}) collective-permute-start(f32[64,1,256]{2,1,0:T(1,128)S(1)} %slice.293), channel_id=1, source_target_pairs={{4,0},{8,4},{12,8},{16,12},{20,16},{24,20},{28,24},{0,28},{5,1},{9... | collective-permute-start | bytes 196616 | tf_op jit(solution)/shard_map/ppermute | solution.py:16
  24.2 1.9 copy-start.2
  27.6 9.0 %collective-permute-start.4 = (f32[1,16,256]{2,1,0:T(8,128)S(1)}, f32[1,16,256]{2,1,0:T(8,128)S(1)}, u32[]{:S(2)}, u32[]{:S(2)}) collective-permute-start(f32[1,16,256]{2,1,0:T(8,128)S(1)} %slice_bitcast_fusion.37), channel_id=1, source_target_pairs={{0,1},{1,2},{2,3},{4,5},{5,6},{6,7},{8,9},{9,10},{10,11},{12,13},{... | collective-permute-start | bytes 49160 | tf_op jit(solution)/shard_map/ppermute | solution.py:10
  32.1 5.6 %collective-permute-start.5 = (f32[1,16,256]{2,1,0:T(8,128)S(1)}, f32[1,16,256]{2,1,0:T(8,128)S(1)}, u32[]{:S(2)}, u32[]{:S(2)}) collective-permute-start(f32[1,16,256]{2,1,0:T(8,128)S(1)} %slice_bitcast_fusion.36), channel_id=1, source_target_pairs={{1,0},{2,1},{3,2},{5,4},{6,5},{7,6},{9,8},{10,9},{11,10},{13,12},{... | collective-permute-start | bytes 49160 | tf_op jit(solution)/shard_map/ppermute | solution.py:10
  33.5 4.4 %collective-permute-start.7 = (f32[64,1,256]{2,1,0:T(1,128)S(1)}, f32[64,1,256]{2,1,0:T(1,128)S(1)}, u32[]{:S(2)}, u32[]{:S(2)}) collective-permute-start(f32[64,1,256]{2,1,0:T(1,128)S(1)} %slice.307), channel_id=1, source_target_pairs={{4,0},{8,4},{12,8},{16,12},{20,16},{24,20},{28,24},{0,28},{5,1},{9... | collective-permute-start | bytes 196616 | tf_op jit(solution)/shard_map/ppermute | solution.py:16
  36.0 4.6 %collective-permute-start.6 = (f32[64,1,256]{2,1,0:T(1,128)S(1)}, f32[64,1,256]{2,1,0:T(1,128)S(1)}, u32[]{:S(2)}, u32[]{:S(2)}) collective-permute-start(f32[64,1,256]{2,1,0:T(1,128)S(1)} %slice.303), channel_id=1, source_target_pairs={{28,0},{0,4},{4,8},{8,12},{12,16},{16,20},{20,24},{24,28},{29,1},{... | collective-permute-start | bytes 196616 | tf_op jit(solution)/shard_map/ppermute | solution.py:16
  43.3 6.8 %collective-permute-start.8 = (f32[1,16,256]{2,1,0:T(8,128)S(1)}, f32[1,16,256]{2,1,0:T(8,128)S(1)}, u32[]{:S(2)}, u32[]{:S(2)}) collective-permute-start(f32[1,16,256]{2,1,0:T(8,128)S(1)} %slice_bitcast_fusion.35), channel_id=1, source_target_pairs={{0,1},{1,2},{2,3},{4,5},{5,6},{6,7},{8,9},{9,10},{10,11},{12,13},{... | collective-permute-start | bytes 49160 | tf_op jit(solution)/shard_map/ppermute | solution.py:10
  47.6 5.6 %collective-permute-start.9 = (f32[1,16,256]{2,1,0:T(8,128)S(1)}, f32[1,16,256]{2,1,0:T(8,128)S(1)}, u32[]{:S(2)}, u32[]{:S(2)}) collective-permute-start(f32[1,16,256]{2,1,0:T(8,128)S(1)} %slice_bitcast_fusion.34), channel_id=1, source_target_pairs={{1,0},{2,1},{3,2},{5,4},{6,5},{7,6},{9,8},{10,9},{11,10},{13,12},{... | collective-permute-start | bytes 49160 | tf_op jit(solution)/shard_map/ppermute | solution.py:10
  49.0 4.3 %collective-permute-start.11 = (f32[64,1,256]{2,1,0:T(1,128)S(1)}, f32[64,1,256]{2,1,0:T(1,128)S(1)}, u32[]{:S(2)}, u32[]{:S(2)}) collective-permute-start(f32[64,1,256]{2,1,0:T(1,128)S(1)} %slice.321), channel_id=1, source_target_pairs={{4,0},{8,4},{12,8},{16,12},{20,16},{24,20},{28,24},{0,28},{5,1},{9... | collective-permute-start | bytes 196616 | tf_op jit(solution)/shard_map/ppermute | solution.py:16
  49.1 4.6 %collective-permute-start.10 = (f32[64,1,256]{2,1,0:T(1,128)S(1)}, f32[64,1,256]{2,1,0:T(1,128)S(1)}, u32[]{:S(2)}, u32[]{:S(2)}) collective-permute-start(f32[64,1,256]{2,1,0:T(1,128)S(1)} %slice.317), channel_id=1, source_target_pairs={{28,0},{0,4},{4,8},{8,12},{12,16},{16,20},{20,24},{24,28},{29,1},{... | collective-permute-start | bytes 196616 | tf_op jit(solution)/shard_map/ppermute | solution.py:16
  56.6 10.1 %collective-permute-start.13 = (f32[1,16,256]{2,1,0:T(8,128)S(1)}, f32[1,16,256]{2,1,0:T(8,128)S(1)}, u32[]{:S(2)}, u32[]{:S(2)}) collective-permute-start(f32[1,16,256]{2,1,0:T(8,128)S(1)} %slice_bitcast_fusion.32), channel_id=1, source_target_pairs={{1,0},{2,1},{3,2},{5,4},{6,5},{7,6},{9,8},{10,9},{11,10},{13,12},{... | collective-permute-start | bytes 49160 | tf_op jit(solution)/shard_map/ppermute | solution.py:10
  57.9 8.8 %collective-permute-start.12 = (f32[1,16,256]{2,1,0:T(8,128)S(1)}, f32[1,16,256]{2,1,0:T(8,128)S(1)}, u32[]{:S(2)}, u32[]{:S(2)}) collective-permute-start(f32[1,16,256]{2,1,0:T(8,128)S(1)} %slice_bitcast_fusion.33), channel_id=1, source_target_pairs={{0,1},{1,2},{2,3},{4,5},{5,6},{6,7},{8,9},{9,10},{10,11},{12,13},{... | collective-permute-start | bytes 49160 | tf_op jit(solution)/shard_map/ppermute | solution.py:10
  63.3 4.8 %collective-permute-start.14 = (f32[64,1,256]{2,1,0:T(1,128)S(1)}, f32[64,1,256]{2,1,0:T(1,128)S(1)}, u32[]{:S(2)}, u32[]{:S(2)}) collective-permute-start(f32[64,1,256]{2,1,0:T(1,128)S(1)} %slice.331), channel_id=1, source_target_pairs={{28,0},{0,4},{4,8},{8,12},{12,16},{16,20},{20,24},{24,28},{29,1},{... | collective-permute-start | bytes 196616 | tf_op jit(solution)/shard_map/ppermute | solution.py:16
  63.5 4.7 %collective-permute-start.15 = (f32[64,1,256]{2,1,0:T(1,128)S(1)}, f32[64,1,256]{2,1,0:T(1,128)S(1)}, u32[]{:S(2)}, u32[]{:S(2)}) collective-permute-start(f32[64,1,256]{2,1,0:T(1,128)S(1)} %slice.335), channel_id=1, source_target_pairs={{4,0},{8,4},{12,8},{16,12},{20,16},{24,20},{28,24},{0,28},{5,1},{9... | collective-permute-start | bytes 196616 | tf_op jit(solution)/shard_map/ppermute | solution.py:16
  68.1 3.3 %copy-start.4 = (s32[1,8]{1,0:T(1,128)S(1)}, s32[1,8]{1,0:T(1,128)}, u32[]{:S(2)}) copy-start(s32[1,8]{1,0:T(1,128)} %param.11) | copy-start | bytes 100
  71.3 142.3 %reduce-scatter.2.cloned.1.call-start = ((), (), s32[]{:S(2)}) async-start(), calls=%async_computation.2 | async-start | bytes 5242880 | tf_op jit(solution)/shard_map/reduce_scatter | solution.py:67
  118.1 16.5 %copy-start.3 = (bf16[1,8,4096,32]{2,3,1,0:T(8,128)(2,1)S(1)}, bf16[1,8,4096,32]{2,3,1,0:T(8,128)(2,1)}, u32[]{:S(2)}) copy-start(bf16[1,8,4096,32]{2,3,1,0:T(8,128)(2,1)} %param.13) | copy-start | bytes 6291460
  120.7 3.8 %collective-permute-start.16 = (bf16[256,32]{0,1:T(8,128)(2,1)S(1)}, bf16[256,32]{0,1:T(8,128)(2,1)S(1)}, u32[]{:S(2)}, u32[]{:S(2)}) collective-permute-start(bf16[256,32]{0,1:T(8,128)(2,1)S(1)} %get-tuple-element.35), channel_id=1, source_target_pairs={{16,0},{20,4},{24,8},{28,12},{0,16},{4,20},{8,24},{12,28},{17,1},{... | collective-permute-start | bytes 49160 | tf_op jit(solution)/shard_map/ppermute | solution.py:16
  122.2 12.3 %collective-permute-start.23 = (bf16[256,32]{0,1:T(8,128)(2,1)S(1)}, bf16[256,32]{0,1:T(8,128)(2,1)S(1)}, u32[]{:S(2)}, u32[]{:S(2)}) collective-permute-start(bf16[256,32]{0,1:T(8,128)(2,1)S(1)} %get-tuple-element.28), channel_id=1, source_target_pairs={{20,0},{24,4},{28,8},{0,12},{4,16},{8,20},{12,24},{16,28},{21,1},{... | collective-permute-start | bytes 49160 | tf_op jit(solution)/shard_map/ppermute | solution.py:16
  122.7 11.8 %collective-permute-start.22 = (bf16[256,32]{0,1:T(8,128)(2,1)S(1)}, bf16[256,32]{0,1:T(8,128)(2,1)S(1)}, u32[]{:S(2)}, u32[]{:S(2)}) collective-permute-start(bf16[256,32]{0,1:T(8,128)(2,1)S(1)} %get-tuple-element.29), channel_id=1, source_target_pairs={{24,0},{28,4},{0,8},{4,12},{8,16},{12,20},{16,24},{20,28},{25,1},{... | collective-permute-start | bytes 49160 | tf_op jit(solution)/shard_map/ppermute | solution.py:16
  123.7 10.8 %collective-permute-start.21 = (bf16[256,32]{0,1:T(8,128)(2,1)S(1)}, bf16[256,32]{0,1:T(8,128)(2,1)S(1)}, u32[]{:S(2)}, u32[]{:S(2)}) collective-permute-start(bf16[256,32]{0,1:T(8,128)(2,1)S(1)} %get-tuple-element.30), channel_id=1, source_target_pairs={{28,0},{0,4},{4,8},{8,12},{12,16},{16,20},{20,24},{24,28},{29,1},{... | collective-permute-start | bytes 49160 | tf_op jit(solution)/shard_map/ppermute | solution.py:16
  124.1 10.4 %collective-permute-start.20 = (bf16[256,32]{0,1:T(8,128)(2,1)S(1)}, bf16[256,32]{0,1:T(8,128)(2,1)S(1)}, u32[]{:S(2)}, u32[]{:S(2)}) collective-permute-start(bf16[256,32]{0,1:T(8,128)(2,1)S(1)} %get-tuple-element.31), channel_id=1, source_target_pairs={{0,0},{4,4},{8,8},{12,12},{16,16},{20,20},{24,24},{28,28},{1,1},{5... | collective-permute-start | bytes 49160 | tf_op jit(solution)/shard_map/ppermute | solution.py:16
  124.5 3.2 %collective-permute-start.17 = (bf16[256,32]{0,1:T(8,128)(2,1)S(1)}, bf16[256,32]{0,1:T(8,128)(2,1)S(1)}, u32[]{:S(2)}, u32[]{:S(2)}) collective-permute-start(bf16[256,32]{0,1:T(8,128)(2,1)S(1)} %get-tuple-element.34), channel_id=1, source_target_pairs={{12,0},{16,4},{20,8},{24,12},{28,16},{0,20},{4,24},{8,28},{13,1},{... | collective-permute-start | bytes 49160 | tf_op jit(solution)/shard_map/ppermute | solution.py:16
  127.7 4.9 %collective-permute-start.18 = (bf16[256,32]{0,1:T(8,128)(2,1)S(1)}, bf16[256,32]{0,1:T(8,128)(2,1)S(1)}, u32[]{:S(2)}, u32[]{:S(2)}) collective-permute-start(bf16[256,32]{0,1:T(8,128)(2,1)S(1)} %get-tuple-element.33), channel_id=1, source_target_pairs={{8,0},{12,4},{16,8},{20,12},{24,16},{28,20},{0,24},{4,28},{9,1},{1... | collective-permute-start | bytes 49160 | tf_op jit(solution)/shard_map/ppermute | solution.py:16
  132.5 1.9 collective-permute-start.19
Sparse Core Ops, SparseCore 0:
  71.5 46.5 all-gather.1
  137.4 76.2 reduce-scatter.1
where the time goes:
time: 223 us
  waiting for transfers between devices  138 us (62%)
  starting transfers between devices  41.7 us (19%)
  between operations  14.6 us (7%)
  other arithmetic  14.4 us (6%)
  local copies, waits for them, and re-layouts  8.73 us (4%)
  matrix products  5.16 us (2%)
    reduce_scatter x1, waiting for transfers between devices, per_device(): lax.psum_scatter(jnp.einsum('kzr,ktr->zt', received, right, preferred_ele...  76.4 us
    all_gather x1, waiting for transfers between devices, per_device(): all_levels = lax.all_gather(lam_half, 'depth', axis=0, tiled=True)  46.6 us
    ppermute x8, starting transfers between devices, from_behind(): lax.ppermute(value, axis, [(source, source + steps) for source in range(i...  24.3 us
    ppermute x16, starting transfers between devices, shifted(): return lax.ppermute(block, axis, route)  17.3 us
    ppermute x16, waiting for transfers between devices, shifted(): return lax.ppermute(block, axis, route)  10.8 us
    mul x3, other arithmetic, per_device(): minus_term = minus * lam  4.8 us
    ppermute x8, waiting for transfers between devices, from_behind(): lax.ppermute(value, axis, [(source, source + steps) for source in range(i...  4.56 us
  transfers between devices with their start and end apart: 26, of which 15 were waited for; matrix products, arithmetic and copies ran while one was open for 1% of the time, Pallas kernels for 0%

commit v1 on v0

--- a/solution.py
+++ b/solution.py
@@ -2,6 +2,28 @@
 import jax.numpy as jnp
 from jax import lax
 from jax.sharding import PartitionSpec as P
+
+
+def in_order(parts, dim):
+    dims = list(parts.shape[1:])
+    dims[dim] *= parts.shape[0]
+    return jnp.moveaxis(parts, 0, dim).reshape(dims)
+
+
+def collect(x, axis, dim):
+    devices = lax.axis_size(axis)
+    pairs = [(i, (i + 1) % devices) for i in range(devices)]
+    back = [(b, a) for a, b in pairs]
+    lower, upper = ([], [])
+    for turn in range(devices - 1):
+        if turn % 2 == 0:
+            lower.append(lax.ppermute(lower[-1] if lower else x, axis, pairs))
+        else:
+            upper.append(lax.ppermute(upper[-1] if upper else x, axis, back))
+    blocks = jnp.stack([*lower[::-1], x, *upper])
+    shift = lax.axis_index(axis) - len(lower)
+    blocks = blocks[(jnp.arange(devices) - shift) % devices]
+    return in_order(blocks, dim)
 
 
 def from_behind(value, axis, steps):
@@ -52,7 +74,7 @@
         lam = sea * (out + lat_terms(plus_term[2], minus_term[2]) + innovations[step])
     lam_half = lam.astype(jnp.bfloat16).reshape(levels_here, tile_cols)
     ranks = tile_ranks[0]
-    all_levels = lax.all_gather(lam_half, "depth", axis=0, tiled=True)
+    all_levels = collect(lam_half, "depth", 0)
     left = row_factors[0]
     width = left.shape[2]
     columns = lax.axis_index("depth") * width + jnp.arange(width, dtype=jnp.int32)

time: 223 us -> 222 us (level)
  waiting for transfers between devices: 138 us -> 127 us
  local copies, waits for them, and re-layouts: 8.73 us -> 13.8 us
  other arithmetic: 14.4 us -> 17.9 us
    all_gather x1 -> x0, waiting for transfers between devices: 46.6 us -> none  [per_device(): all_levels = lax.all_gather(lam_half, 'depth', axis=0, tiled=True)]
    ppermute x0 -> x3, waiting for transfers between devices: none -> 32.8 us  [the longest x2 23.4 us: collect(): lower.append(lax.ppermute(lower[-1] if lower else x, axis, pairs))]
    ppermute x0 -> x3, starting transfers between devices: none -> 4.01 us  [the longest x2 2.2 us: collect(): lower.append(lax.ppermute(lower[-1] if lower else x, axis, pairs))]
    gather x0 -> x1, local copies, waits for them, and re-layouts: none -> 3.6 us  [collect(): blocks = blocks[(jnp.arange(devices) - shift) % devices]]
    ppermute x16, starting transfers between devices: 17.3 us -> 14.1 us  [shifted(): return lax.ppermute(block, axis, route)]
    another operation x0 -> x1, other arithmetic: none -> 2.96 us  [collect(): blocks = jnp.stack([*lower[::-1], x, *upper])]
  transfers between devices with their start and end apart: 26 -> 28, of which waited for: 15 -> 17; matrix products, arithmetic and copies ran while one was open for 1% -> 2% of each run, Pallas kernels for 0% -> 0%
where the time goes in v1:
time: 222 us; the launch traced here: 221 us
  waiting for transfers between devices  127 us (57%)
  starting transfers between devices  42.5 us (19%)
  other arithmetic  17.9 us (8%)
  between operations  14.6 us (7%)
  local copies, waits for them, and re-layouts  13.8 us (6%)
  matrix products  5.17 us (2%)
    reduce_scatter x1, waiting for transfers between devices, per_device(): lax.psum_scatter(jnp.einsum('kzr,ktr->zt', received, right, preferred_ele...  76.8 us
    ppermute x8, starting transfers between devices, from_behind(): lax.ppermute(value, axis, [(source, source + steps) for source in range(i...  24.3 us
    ppermute x2, waiting for transfers between devices, collect(): lower.append(lax.ppermute(lower[-1] if lower else x, axis, pairs))  23.4 us
    ppermute x16, starting transfers between devices, shifted(): return lax.ppermute(block, axis, route)  14.1 us
    ppermute x16, waiting for transfers between devices, shifted(): return lax.ppermute(block, axis, route)  12.8 us
    ppermute x1, waiting for transfers between devices, collect(): upper.append(lax.ppermute(upper[-1] if upper else x, axis, back))  9.4 us
    mul x3, other arithmetic, per_device(): minus_term = minus * lam  5.12 us
    ppermute x8, waiting for transfers between devices, from_behind(): lax.ppermute(value, axis, [(source, source + steps) for source in range(i...  4.59 us
  transfers between devices with their start and end apart: 28, of which 17 were waited for; matrix products, arithmetic and copies ran while one was open for 2% of the time, Pallas kernels for 0%

profile of v1, /device:TPU:0, one launch (start us, length us, event | category | flops | bytes accessed | tf_op | source)
XLA Modules:
  0.0 220.9 jit_solution(13519758287987550850)
XLA Ops:
  7.2 1.0 convert_element_type.29
  8.4 1.4 multiply_bitcast_fusion
  9.8 2.8 %fusion.8 = (f32[3,64,16,256]{3,2,1,0:T(8,128)S(1)}, f32[3,64,16,256]{3,2,1,0:T(8,128)S(1)}) fusion(f32[3,64,16,256]{3,2,1,0:T(8,128)} %param.8, f32[64,16,256]{2,1,0:T(8,128)S(1)} %multiply_bitcast_fusion, f32[64,16,256]{2,1,0:T(8,128)S(1)} %copy-done.1), kind=kLoop, calls=%fused_computation.13 | loop fusion | flops 3932160 | bytes 11534336 | tf_op jit(solution)/shard_map/mul | solution.py:64
  12.7 5.0 %collective-permute-start = (f32[1,16,256]{2,1,0:T(8,128)S(1)}, f32[1,16,256]{2,1,0:T(8,128)S(1)}, u32[]{:S(2)}, u32[]{:S(2)}) collective-permute-start(f32[1,16,256]{2,1,0:T(8,128)S(1)} %slice_bitcast_fusion.39), channel_id=1, source_target_pairs={{0,1},{1,2},{2,3},{4,5},{5,6},{6,7},{8,9},{9,10},{10,11},{12,13},{... | collective-permute-start | bytes 49160 | tf_op jit(solution)/shard_map/ppermute | solution.py:32
  17.7 1.3 collective-permute-start.1
  19.6 2.7 %collective-permute-start.3 = (f32[64,1,256]{2,1,0:T(1,128)S(1)}, f32[64,1,256]{2,1,0:T(1,128)S(1)}, u32[]{:S(2)}, u32[]{:S(2)}) collective-permute-start(f32[64,1,256]{2,1,0:T(1,128)S(1)} %slice.295), channel_id=1, source_target_pairs={{4,0},{8,4},{12,8},{16,12},{20,16},{24,20},{28,24},{0,28},{5,1},{9... | collective-permute-start | bytes 196616 | tf_op jit(solution)/shard_map/ppermute | solution.py:38
  23.3 0.9 collective-permute-done.2
  24.2 1.3 fusion.14
  25.5 0.6 copy-done.2
  26.1 1.1 fusion.7
  27.7 4.5 %collective-permute-start.4 = (f32[1,16,256]{2,1,0:T(8,128)S(1)}, f32[1,16,256]{2,1,0:T(8,128)S(1)}, u32[]{:S(2)}, u32[]{:S(2)}) collective-permute-start(f32[1,16,256]{2,1,0:T(8,128)S(1)} %slice_bitcast_fusion.37), channel_id=1, source_target_pairs={{0,1},{1,2},{2,3},{4,5},{5,6},{6,7},{8,9},{9,10},{10,11},{12,13},{... | collective-permute-start | bytes 49160 | tf_op jit(solution)/shard_map/ppermute | solution.py:32
  32.3 1.3 collective-permute-start.5
  33.6 2.5 %collective-permute-start.7 = (f32[64,1,256]{2,1,0:T(1,128)S(1)}, f32[64,1,256]{2,1,0:T(1,128)S(1)}, u32[]{:S(2)}, u32[]{:S(2)}) collective-permute-start(f32[64,1,256]{2,1,0:T(1,128)S(1)} %slice.309), channel_id=1, source_target_pairs={{4,0},{8,4},{12,8},{16,12},{20,16},{24,20},{28,24},{0,28},{5,1},{9... | collective-permute-start | bytes 196616 | tf_op jit(solution)/shard_map/ppermute | solution.py:38
  36.7 1.2 collective-permute-done.5
  38.0 2.8 %collective-permute-done.6 = f32[64,1,256]{2,1,0:T(1,128)S(1)} collective-permute-done((f32[64,1,256]{2,1,0:T(1,128)S(1)}, f32[64,1,256]{2,1,0:T(1,128)S(1)}, u32[]{:S(2)}, u32[]{:S(2)}) %collective-permute-start.6) | collective-permute-done | bytes 65568 | tf_op jit(solution)/shard_map/ppermute | solution.py:38
  40.8 1.2 fusion.20
  42.0 1.1 fusion.6
  43.6 4.3 %collective-permute-start.8 = (f32[1,16,256]{2,1,0:T(8,128)S(1)}, f32[1,16,256]{2,1,0:T(8,128)S(1)}, u32[]{:S(2)}, u32[]{:S(2)}) collective-permute-start(f32[1,16,256]{2,1,0:T(8,128)S(1)} %slice_bitcast_fusion.35), channel_id=1, source_target_pairs={{0,1},{1,2},{2,3},{4,5},{5,6},{6,7},{8,9},{9,10},{10,11},{12,13},{... | collective-permute-start | bytes 49160 | tf_op jit(solution)/shard_map/ppermute | solution.py:32
  47.9 1.3 collective-permute-start.9
  49.4 0.5 collective-permute-start.10
  50.5 3.1 %collective-permute-done.9 = f32[1,16,256]{2,1,0:T(8,128)S(1)} collective-permute-done((f32[1,16,256]{2,1,0:T(8,128)S(1)}, f32[1,16,256]{2,1,0:T(8,128)S(1)}, u32[]{:S(2)}, u32[]{:S(2)}) %collective-permute-start.9) | collective-permute-done | bytes 16416 | tf_op jit(solution)/shard_map/ppermute | solution.py:32
  54.0 1.2 fusion.26
  55.3 1.1 fusion.1
  56.9 1.3 collective-permute-start.13
  58.2 5.4 %collective-permute-start.12 = (f32[1,16,256]{2,1,0:T(8,128)S(1)}, f32[1,16,256]{2,1,0:T(8,128)S(1)}, u32[]{:S(2)}, u32[]{:S(2)}) collective-permute-start(f32[1,16,256]{2,1,0:T(8,128)S(1)} %slice_bitcast_fusion.33), channel_id=1, source_target_pairs={{0,1},{1,2},{2,3},{4,5},{5,6},{6,7},{8,9},{9,10},{10,11},{12,13},{... | collective-permute-start | bytes 49160 | tf_op jit(solution)/shard_map/ppermute | solution.py:32
  63.8 2.7 %collective-permute-start.15 = (f32[64,1,256]{2,1,0:T(1,128)S(1)}, f32[64,1,256]{2,1,0:T(1,128)S(1)}, u32[]{:S(2)}, u32[]{:S(2)}) collective-permute-start(f32[64,1,256]{2,1,0:T(1,128)S(1)} %slice.337), channel_id=1, source_target_pairs={{4,0},{8,4},{12,8},{16,12},{20,16},{24,20},{28,24},{0,28},{5,1},{9... | collective-permute-start | bytes 196616 | tf_op jit(solution)/shard_map/ppermute | solution.py:38
  67.0 1.4 collective-permute-done.14
  68.4 2.4 %fusion.37 = (bf16[64,16,256]{2,1,0:T(8,128)(2,1)}, f32[64,16,256]{2,1,0:T(8,128)}) fusion(f32[5,64,16,256]{3,2,1,0:T(8,128)S(1)} %bitcast.153, f32[64,16,255]{2,1,0:T(8,128)S(1)} %slice.341, f32[64,16,255]{2,1,0:T(8,128)S(1)} %bitcast.158, f32[64,1,256]{2,1,0:T(1,128)S(1)} %collective-permute-done.15, f32[64,15,256]{2,1,0:T(8,128)S(1)} %slice.336, ...), kind=kLoop, calls=%fused_computation.105 | loop fusion | flops 4194304 | bytes 11067392 | tf_op jit(solution)/shard_map/convert_element_type | solution.py:75
  70.8 1.2 copy.12
  72.0 2.1 collective-permute-start.16
  74.1 1.8 collective-permute-start.18
  75.9 13.0 %collective-permute-done.16 = bf16[64,4096]{1,0:T(8,128)(2,1)} collective-permute-done((bf16[64,4096]{1,0:T(8,128)(2,1)S(1)}, bf16[64,4096]{1,0:T(8,128)(2,1)}, u32[]{:S(2)}, u32[]{:S(2)}) %collective-permute-start.16) | collective-permute-done | bytes 524320 | tf_op jit(solution)/shard_map/ppermute | solution.py:20
  89.1 1.3 stack_reshape.3
  90.4 9.4 %collective-permute-done.18 = bf16[64,4096]{1,0:T(8,128)(2,1)} collective-permute-done((bf16[64,4096]{1,0:T(8,128)(2,1)S(1)}, bf16[64,4096]{1,0:T(8,128)(2,1)}, u32[]{:S(2)}, u32[]{:S(2)}) %collective-permute-start.18) | collective-permute-done | bytes 524320 | tf_op jit(solution)/shard_map/ppermute | solution.py:22
  99.8 10.4 %collective-permute-done.17 = bf16[64,4096]{1,0:T(8,128)(2,1)} collective-permute-done((bf16[64,4096]{1,0:T(8,128)(2,1)}, bf16[64,4096]{1,0:T(8,128)(2,1)}, u32[]{:S(2)}, u32[]{:S(2)}) %collective-permute-start.17) | collective-permute-done | bytes 524320 | tf_op jit(solution)/shard_map/ppermute | solution.py:20
  110.2 3.0 %pad_maximum_fusion = bf16[4,64,4096]{2,1,0:T(8,128)(2,1)} fusion(bf16[1,64,4096]{2,1,0:T(8,128)(2,1)} %bitcast.42, bf16[1,64,4096]{2,1,0:T(8,128)(2,1)S(1)} %stack_reshape.3, bf16[1,64,4096]{2,1,0:T(8,128)(2,1)} %bitcast.41, bf16[1,64,4096]{2,1,0:T(8,128)(2,1)} %bitcast.40), kind=kLoop, calls=%fused_computation.4 | loop fusion | flops 3145728 | bytes 4194304 | tf_op jit(solution)/shard_map/stack | solution.py:23
  113.2 3.6 %gather_fusion = bf16[4,64,4096]{2,1,0:T(8,128)(2,1)} fusion(bf16[4,64,4096]{2,1,0:T(8,128)(2,1)} %pad_maximum_fusion, s32[1024]{0:T(1024)S(1)} %pad_clamp_fusion), kind=kCustom, calls=%fused_computation | custom fusion | bytes 4194320 | tf_op jit(solution)/shard_map/gather | solution.py:25
  116.8 2.5 %fusion.39 = f32[256,256]{0,1:S(1)} fusion(bf16[256,4096]{1,0:T(8,128)(2,1)} %bitcast.151, bf16[4096,256]{0,1:T(8,128)(2,1)S(1)} %bitcast.150), kind=kOutput, calls=%fused_computation.106 | convolution fusion | flops 536870912 | bytes 4456448
  119.4 1.5 collective-permute-start.19
  121.6 1.6 collective-permute-done.19
  123.2 0.9 collective-permute-start.20
  124.1 2.3 %collective-permute-done.20 = bf16[256,32]{0,1:T(8,128)(2,1)S(1)} collective-permute-done((bf16[256,32]{0,1:T(8,128)(2,1)S(1)}, bf16[256,32]{0,1:T(8,128)(2,1)S(1)}, u32[]{:S(2)}, u32[]{:S(2)}) %collective-permute-start.20) | collective-permute-done | bytes 16416 | tf_op jit(solution)/shard_map/ppermute | solution.py:38
  126.4 2.0 collective-permute-start.21
  128.3 1.8 collective-permute-done.21
  130.6 1.4 collective-permute-done.22
  132.1 2.7 %convolution_bitcast_fusion = f32[256,4096]{1,0:T(8,128)} fusion(bf16[8,256,32]{1,2,0:T(8,128)(2,1)S(1)} %constant_dynamic-update-slice_fusion, bf16[1,8,4096,32]{2,3,1,0:T(8,128)(2,1)S(1)} %copy-done.3), kind=kOutput, calls=%fused_computation.1 | convolution fusion | flops 536870912 | bytes 6422528 | tf_op jit(solution)/shard_map/kzr,ktr->zt/dot_general | solution.py:90
  134.8 76.8 %reduce-scatter.2.cloned.1.call-done = f32[64,4096]{1,0:T(8,128)} async-done(((f32[256,4096]{1,0:T(8,128)}), f32[64,4096]{1,0:T(8,128)}) %reduce-scatter.2.cloned.1.call-update) | async-done | bytes 1048592 | tf_op jit(solution)/shard_map/reduce_scatter | solution.py:89
  211.6 2.5 %copy.13 = f32[8,8,16,256]{3,2,1,0:T(8,128)} copy(f32[8,8,16,256]{3,1,2,0:T(8,128)} %bitcast.164) | data formatting | bytes 2097152
  (96 shorter events, 7.4 us)
Async XLA Ops:
  7.2 109.6 %copy-start = (bf16[1,8,4096,32]{2,3,1,0:T(8,128)(2,1)S(1)}, bf16[1,8,4096,32]{2,3,1,0:T(8,128)(2,1)}, u32[]{:S(2)}) copy-start(bf16[1,8,4096,32]{2,3,1,0:T(8,128)(2,1)} %param.12) | copy-start | bytes 6291460
  7.2 2.6 %copy-start.1 = (f32[64,16,256]{2,1,0:T(8,128)S(1)}, f32[64,16,256]{2,1,0:T(8,128)}, u32[]{:S(2)}) copy-start(f32[64,16,256]{2,1,0:T(8,128)} %param.9) | copy-start | bytes 3145732
  7.2 204.4 %reduce-scatter.2.cloned.1.call-start = ((), (), s32[]{:S(2)}) async-start(), calls=%async_computation.1 | async-start | bytes 5242880 | tf_op jit(solution)/shard_map/reduce_scatter | solution.py:89
  12.7 10.2 %collective-permute-start = (f32[1,16,256]{2,1,0:T(8,128)S(1)}, f32[1,16,256]{2,1,0:T(8,128)S(1)}, u32[]{:S(2)}, u32[]{:S(2)}) collective-permute-start(f32[1,16,256]{2,1,0:T(8,128)S(1)} %slice_bitcast_fusion.39), channel_id=1, source_target_pairs={{0,1},{1,2},{2,3},{4,5},{5,6},{6,7},{8,9},{9,10},{10,11},{12,13},{... | collective-permute-start | bytes 49160 | tf_op jit(solution)/shard_map/ppermute | solution.py:32
  17.7 5.6 %collective-permute-start.1 = (f32[1,16,256]{2,1,0:T(8,128)S(1)}, f32[1,16,256]{2,1,0:T(8,128)S(1)}, u32[]{:S(2)}, u32[]{:S(2)}) collective-permute-start(f32[1,16,256]{2,1,0:T(8,128)S(1)} %slice_bitcast_fusion.38), channel_id=1, source_target_pairs={{1,0},{2,1},{3,2},{5,4},{6,5},{7,6},{9,8},{10,9},{11,10},{13,12},{... | collective-permute-start | bytes 49160 | tf_op jit(solution)/shard_map/ppermute | solution.py:32
  19.0 5.2 %slice-start = ((s8[5242880]{0:T(1024)(128)(4,1)}), s8[4194304]{0:T(1024)(128)(4,1)S(1)}, s32[]{:S(2)}) async-start(s8[5242880]{0:T(1024)(128)(4,1)} %bitcast.152), calls=%async_computation.2 | async-start | bytes 8388608
  19.4 4.8 %slice-start.1 = ((s8[5242880]{0:T(1024)(128)(4,1)}), s8[1048576]{0:T(1024)(128)(4,1)S(1)}, s32[]{:S(2)}) async-start(s8[5242880]{0:T(1024)(128)(4,1)} %bitcast.152), calls=%async_computation.3 | async-start | bytes 2097152
  19.5 4.6 %collective-permute-start.2 = (f32[64,1,256]{2,1,0:T(1,128)S(1)}, f32[64,1,256]{2,1,0:T(1,128)S(1)}, u32[]{:S(2)}, u32[]{:S(2)}) collective-permute-start(f32[64,1,256]{2,1,0:T(1,128)S(1)} %slice.291), channel_id=1, source_target_pairs={{28,0},{0,4},{4,8},{8,12},{12,16},{16,20},{20,24},{24,28},{29,1},{... | collective-permute-start | bytes 196616 | tf_op jit(solution)/shard_map/ppermute | solution.py:38
  19.6 4.6 %collective-permute-start.3 = (f32[64,1,256]{2,1,0:T(1,128)S(1)}, f32[64,1,256]{2,1,0:T(1,128)S(1)}, u32[]{:S(2)}, u32[]{:S(2)}) collective-permute-start(f32[64,1,256]{2,1,0:T(1,128)S(1)} %slice.295), channel_id=1, source_target_pairs={{4,0},{8,4},{12,8},{16,12},{20,16},{24,20},{28,24},{0,28},{5,1},{9... | collective-permute-start | bytes 196616 | tf_op jit(solution)/shard_map/ppermute | solution.py:38
  24.2 1.9 copy-start.2
  27.7 9.0 %collective-permute-start.4 = (f32[1,16,256]{2,1,0:T(8,128)S(1)}, f32[1,16,256]{2,1,0:T(8,128)S(1)}, u32[]{:S(2)}, u32[]{:S(2)}) collective-permute-start(f32[1,16,256]{2,1,0:T(8,128)S(1)} %slice_bitcast_fusion.37), channel_id=1, source_target_pairs={{0,1},{1,2},{2,3},{4,5},{5,6},{6,7},{8,9},{9,10},{10,11},{12,13},{... | collective-permute-start | bytes 49160 | tf_op jit(solution)/shard_map/ppermute | solution.py:32
  32.3 5.6 %collective-permute-start.5 = (f32[1,16,256]{2,1,0:T(8,128)S(1)}, f32[1,16,256]{2,1,0:T(8,128)S(1)}, u32[]{:S(2)}, u32[]{:S(2)}) collective-permute-start(f32[1,16,256]{2,1,0:T(8,128)S(1)} %slice_bitcast_fusion.36), channel_id=1, source_target_pairs={{1,0},{2,1},{3,2},{5,4},{6,5},{7,6},{9,8},{10,9},{11,10},{13,12},{... | collective-permute-start | bytes 49160 | tf_op jit(solution)/shard_map/ppermute | solution.py:32
  33.6 4.4 %collective-permute-start.7 = (f32[64,1,256]{2,1,0:T(1,128)S(1)}, f32[64,1,256]{2,1,0:T(1,128)S(1)}, u32[]{:S(2)}, u32[]{:S(2)}) collective-permute-start(f32[64,1,256]{2,1,0:T(1,128)S(1)} %slice.309), channel_id=1, source_target_pairs={{4,0},{8,4},{12,8},{16,12},{20,16},{24,20},{28,24},{0,28},{5,1},{9... | collective-permute-start | bytes 196616 | tf_op jit(solution)/shard_map/ppermute | solution.py:38
  36.1 4.6 %collective-permute-start.6 = (f32[64,1,256]{2,1,0:T(1,128)S(1)}, f32[64,1,256]{2,1,0:T(1,128)S(1)}, u32[]{:S(2)}, u32[]{:S(2)}) collective-permute-start(f32[64,1,256]{2,1,0:T(1,128)S(1)} %slice.305), channel_id=1, source_target_pairs={{28,0},{0,4},{4,8},{8,12},{12,16},{16,20},{20,24},{24,28},{29,1},{... | collective-permute-start | bytes 196616 | tf_op jit(solution)/shard_map/ppermute | solution.py:38
  43.6 6.8 %collective-permute-start.8 = (f32[1,16,256]{2,1,0:T(8,128)S(1)}, f32[1,16,256]{2,1,0:T(8,128)S(1)}, u32[]{:S(2)}, u32[]{:S(2)}) collective-permute-start(f32[1,16,256]{2,1,0:T(8,128)S(1)} %slice_bitcast_fusion.35), channel_id=1, source_target_pairs={{0,1},{1,2},{2,3},{4,5},{5,6},{6,7},{8,9},{9,10},{10,11},{12,13},{... | collective-permute-start | bytes 49160 | tf_op jit(solution)/shard_map/ppermute | solution.py:32
  47.9 5.6 %collective-permute-start.9 = (f32[1,16,256]{2,1,0:T(8,128)S(1)}, f32[1,16,256]{2,1,0:T(8,128)S(1)}, u32[]{:S(2)}, u32[]{:S(2)}) collective-permute-start(f32[1,16,256]{2,1,0:T(8,128)S(1)} %slice_bitcast_fusion.34), channel_id=1, source_target_pairs={{1,0},{2,1},{3,2},{5,4},{6,5},{7,6},{9,8},{10,9},{11,10},{13,12},{... | collective-permute-start | bytes 49160 | tf_op jit(solution)/shard_map/ppermute | solution.py:32
  49.3 4.3 %collective-permute-start.11 = (f32[64,1,256]{2,1,0:T(1,128)S(1)}, f32[64,1,256]{2,1,0:T(1,128)S(1)}, u32[]{:S(2)}, u32[]{:S(2)}) collective-permute-start(f32[64,1,256]{2,1,0:T(1,128)S(1)} %slice.323), channel_id=1, source_target_pairs={{4,0},{8,4},{12,8},{16,12},{20,16},{24,20},{28,24},{0,28},{5,1},{9... | collective-permute-start | bytes 196616 | tf_op jit(solution)/shard_map/ppermute | solution.py:38
  49.4 4.6 %collective-permute-start.10 = (f32[64,1,256]{2,1,0:T(1,128)S(1)}, f32[64,1,256]{2,1,0:T(1,128)S(1)}, u32[]{:S(2)}, u32[]{:S(2)}) collective-permute-start(f32[64,1,256]{2,1,0:T(1,128)S(1)} %slice.319), channel_id=1, source_target_pairs={{28,0},{0,4},{4,8},{8,12},{12,16},{16,20},{20,24},{24,28},{29,1},{... | collective-permute-start | bytes 196616 | tf_op jit(solution)/shard_map/ppermute | solution.py:38
  56.9 10.1 %collective-permute-start.13 = (f32[1,16,256]{2,1,0:T(8,128)S(1)}, f32[1,16,256]{2,1,0:T(8,128)S(1)}, u32[]{:S(2)}, u32[]{:S(2)}) collective-permute-start(f32[1,16,256]{2,1,0:T(8,128)S(1)} %slice_bitcast_fusion.32), channel_id=1, source_target_pairs={{1,0},{2,1},{3,2},{5,4},{6,5},{7,6},{9,8},{10,9},{11,10},{13,12},{... | collective-permute-start | bytes 49160 | tf_op jit(solution)/shard_map/ppermute | solution.py:32
  58.2 8.8 %collective-permute-start.12 = (f32[1,16,256]{2,1,0:T(8,128)S(1)}, f32[1,16,256]{2,1,0:T(8,128)S(1)}, u32[]{:S(2)}, u32[]{:S(2)}) collective-permute-start(f32[1,16,256]{2,1,0:T(8,128)S(1)} %slice_bitcast_fusion.33), channel_id=1, source_target_pairs={{0,1},{1,2},{2,3},{4,5},{5,6},{6,7},{8,9},{9,10},{10,11},{12,13},{... | collective-permute-start | bytes 49160 | tf_op jit(solution)/shard_map/ppermute | solution.py:32
  63.6 4.8 %collective-permute-start.14 = (f32[64,1,256]{2,1,0:T(1,128)S(1)}, f32[64,1,256]{2,1,0:T(1,128)S(1)}, u32[]{:S(2)}, u32[]{:S(2)}) collective-permute-start(f32[64,1,256]{2,1,0:T(1,128)S(1)} %slice.333), channel_id=1, source_target_pairs={{28,0},{0,4},{4,8},{8,12},{12,16},{16,20},{20,24},{24,28},{29,1},{... | collective-permute-start | bytes 196616 | tf_op jit(solution)/shard_map/ppermute | solution.py:38
  63.8 4.7 %collective-permute-start.15 = (f32[64,1,256]{2,1,0:T(1,128)S(1)}, f32[64,1,256]{2,1,0:T(1,128)S(1)}, u32[]{:S(2)}, u32[]{:S(2)}) collective-permute-start(f32[64,1,256]{2,1,0:T(1,128)S(1)} %slice.337), channel_id=1, source_target_pairs={{4,0},{8,4},{12,8},{16,12},{20,16},{24,20},{28,24},{0,28},{5,1},{9... | collective-permute-start | bytes 196616 | tf_op jit(solution)/shard_map/ppermute | solution.py:38
  68.4 20.6 %copy-start.4 = (s32[1,8]{1,0:T(1,128)S(1)}, s32[1,8]{1,0:T(1,128)}, u32[]{:S(2)}) copy-start(s32[1,8]{1,0:T(1,128)} %param.11) | copy-start | bytes 100
  72.0 16.8 %collective-permute-start.16 = (bf16[64,4096]{1,0:T(8,128)(2,1)S(1)}, bf16[64,4096]{1,0:T(8,128)(2,1)}, u32[]{:S(2)}, u32[]{:S(2)}) collective-permute-start(bf16[64,4096]{1,0:T(8,128)(2,1)S(1)} %bitcast.166), channel_id=1, source_target_pairs={{0,1},{1,2},{2,3},{3,0},{4,5},{5,6},{6,7},{7,4},{8,9},{9,10},{10,1... | collective-permute-start | bytes 1572872 | tf_op jit(solution)/shard_map/ppermute | solution.py:20
  74.1 25.7 %collective-permute-start.18 = (bf16[64,4096]{1,0:T(8,128)(2,1)S(1)}, bf16[64,4096]{1,0:T(8,128)(2,1)}, u32[]{:S(2)}, u32[]{:S(2)}) collective-permute-start(bf16[64,4096]{1,0:T(8,128)(2,1)S(1)} %bitcast.167), channel_id=1, source_target_pairs={{1,0},{2,1},{3,2},{0,3},{5,4},{6,5},{7,6},{4,7},{9,8},{10,9},{11,1... | collective-permute-start | bytes 1572872 | tf_op jit(solution)/shard_map/ppermute | solution.py:22
  88.9 21.3 %collective-permute-start.17 = (bf16[64,4096]{1,0:T(8,128)(2,1)}, bf16[64,4096]{1,0:T(8,128)(2,1)}, u32[]{:S(2)}, u32[]{:S(2)}) collective-permute-start(bf16[64,4096]{1,0:T(8,128)(2,1)} %collective-permute-done.16), channel_id=1, source_target_pairs={{0,1},{1,2},{2,3},{3,0},{4,5},{5,6},{6,7},{7,4},{8,9},{9,10},{10,1... | collective-permute-start | bytes 1572872 | tf_op jit(solution)/shard_map/ppermute | solution.py:20
  116.8 15.3 %copy-start.3 = (bf16[1,8,4096,32]{2,3,1,0:T(8,128)(2,1)S(1)}, bf16[1,8,4096,32]{2,3,1,0:T(8,128)(2,1)}, u32[]{:S(2)}) copy-start(bf16[1,8,4096,32]{2,3,1,0:T(8,128)(2,1)} %param.13) | copy-start | bytes 6291460
  119.4 3.8 %collective-permute-start.19 = (bf16[256,32]{0,1:T(8,128)(2,1)S(1)}, bf16[256,32]{0,1:T(8,128)(2,1)S(1)}, u32[]{:S(2)}, u32[]{:S(2)}) collective-permute-start(bf16[256,32]{0,1:T(8,128)(2,1)S(1)} %get-tuple-element.35), channel_id=1, source_target_pairs={{16,0},{20,4},{24,8},{28,12},{0,16},{4,20},{8,24},{12,28},{17,1},{... | collective-permute-start | bytes 49160 | tf_op jit(solution)/shard_map/ppermute | solution.py:38
  120.9 11.2 %collective-permute-start.26 = (bf16[256,32]{0,1:T(8,128)(2,1)S(1)}, bf16[256,32]{0,1:T(8,128)(2,1)S(1)}, u32[]{:S(2)}, u32[]{:S(2)}) collective-permute-start(bf16[256,32]{0,1:T(8,128)(2,1)S(1)} %get-tuple-element.28), channel_id=1, source_target_pairs={{20,0},{24,4},{28,8},{0,12},{4,16},{8,20},{12,24},{16,28},{21,1},{... | collective-permute-start | bytes 49160 | tf_op jit(solution)/shard_map/ppermute | solution.py:38
  120.9 11.2 %collective-permute-start.25 = (bf16[256,32]{0,1:T(8,128)(2,1)S(1)}, bf16[256,32]{0,1:T(8,128)(2,1)S(1)}, u32[]{:S(2)}, u32[]{:S(2)}) collective-permute-start(bf16[256,32]{0,1:T(8,128)(2,1)S(1)} %get-tuple-element.29), channel_id=1, source_target_pairs={{24,0},{28,4},{0,8},{4,12},{8,16},{12,20},{16,24},{20,28},{25,1},{... | collective-permute-start | bytes 49160 | tf_op jit(solution)/shard_map/ppermute | solution.py:38
  121.3 10.8 %collective-permute-start.24 = (bf16[256,32]{0,1:T(8,128)(2,1)S(1)}, bf16[256,32]{0,1:T(8,128)(2,1)S(1)}, u32[]{:S(2)}, u32[]{:S(2)}) collective-permute-start(bf16[256,32]{0,1:T(8,128)(2,1)S(1)} %get-tuple-element.30), channel_id=1, source_target_pairs={{28,0},{0,4},{4,8},{8,12},{12,16},{16,20},{20,24},{24,28},{29,1},{... | collective-permute-start | bytes 49160 | tf_op jit(solution)/shard_map/ppermute | solution.py:38
  121.6 10.4 %collective-permute-start.23 = (bf16[256,32]{0,1:T(8,128)(2,1)S(1)}, bf16[256,32]{0,1:T(8,128)(2,1)S(1)}, u32[]{:S(2)}, u32[]{:S(2)}) collective-permute-start(bf16[256,32]{0,1:T(8,128)(2,1)S(1)} %get-tuple-element.31), channel_id=1, source_target_pairs={{0,0},{4,4},{8,8},{12,12},{16,16},{20,20},{24,24},{28,28},{1,1},{5... | collective-permute-start | bytes 49160 | tf_op jit(solution)/shard_map/ppermute | solution.py:38
  123.2 3.2 %collective-permute-start.20 = (bf16[256,32]{0,1:T(8,128)(2,1)S(1)}, bf16[256,32]{0,1:T(8,128)(2,1)S(1)}, u32[]{:S(2)}, u32[]{:S(2)}) collective-permute-start(bf16[256,32]{0,1:T(8,128)(2,1)S(1)} %get-tuple-element.34), channel_id=1, source_target_pairs={{12,0},{16,4},{20,8},{24,12},{28,16},{0,20},{4,24},{8,28},{13,1},{... | collective-permute-start | bytes 49160 | tf_op jit(solution)/shard_map/ppermute | solution.py:38
  126.4 3.7 %collective-permute-start.21 = (bf16[256,32]{0,1:T(8,128)(2,1)S(1)}, bf16[256,32]{0,1:T(8,128)(2,1)S(1)}, u32[]{:S(2)}, u32[]{:S(2)}) collective-permute-start(bf16[256,32]{0,1:T(8,128)(2,1)S(1)} %get-tuple-element.33), channel_id=1, source_target_pairs={{8,0},{12,4},{16,8},{20,12},{24,16},{28,20},{0,24},{4,28},{9,1},{1... | collective-permute-start | bytes 49160 | tf_op jit(solution)/shard_map/ppermute | solution.py:38
  130.1 1.9 collective-permute-start.22
Sparse Core Ops, SparseCore 0:
  134.9 76.5 reduce-scatter.1
